TPU v7x, 512 devices: a whole 4x8x8 slice. The times are simulated.
512 devices in a mesh: occ: 8 (over z), vir: 64 (over y, x, core).
Axes of the slice: x: 4, y: 8, z: 8, core: 2. Of those that a mesh axis runs over, the one named last changes fastest.
Arguments:
- amplitudes: bfloat16 [6144, 2048], P('occ', 'vir'), may hold values from -6 to 6
- integrals: bfloat16 [2048, 163840], P('occ', 'vir'), may hold values from -0.375 to 0.375
- occ_sym: int32 [48], P('occ'), may hold values from 0 to 7, as said below
- vir_sym: int32 [1280], P('vir'), may hold values from 0 to 7, as said below
- k_sym: int32 [16], replicated, may hold values from 0 to 7
Outputs:
- ladder: bfloat16 [6144, 163840], P('occ', 'vir')
Inputs may be any that keep to these rules, and one draw needn't show every extreme that they name: `occ_sym`: among the 6 blocks of one index of occ no irrep occurs more than 2 times, and one occurs exactly 2 times. `vir_sym`: among the 20 blocks of one index of vir no irrep occurs more than 5 times, and one occurs exactly 5 times.
All inputs are finite; a program needn't handle non-finite values.
Results may differ from a plain program's by a relative error of at most 0.001.
Values may be sent and summed in bfloat16 or wider, within the bound.
A program may use at most 64 MiB of HBM per device.

v0:
```python
import jax
import jax.numpy as jnp
from jax import lax
from jax.sharding import PartitionSpec as P

BLK = 128
MAXB = 5


def slot_order(symmetry, labels, slot_bound):
    label_count = labels.shape[0]
    positions = jnp.arange(label_count, dtype=jnp.int32)
    matching = labels == symmetry
    ranking = jnp.where(matching, positions, positions + label_count)
    chosen = jnp.argsort(ranking)[:slot_bound]
    return (chosen, matching[chosen])


def slot_table(symmetry, labels, slot_bound):
    chosen, usable = slot_order(symmetry, labels, slot_bound)
    positions = jnp.arange(labels.shape[0], dtype=jnp.int32)
    return ((chosen[:, None] == positions[None, :]) & usable[:, None]).astype(jnp.bfloat16)


def per_device(amplitudes, integrals, occ_sym, vir_sym, k_sym):
    occ_rows = amplitudes.shape[0]
    occ_blocks = occ_rows // BLK
    kblocks = k_sym.shape[0]
    window = kblocks * BLK
    vir_blocks = vir_sym.shape[0]
    col_width = vir_blocks * BLK
    block_ids = jnp.arange(kblocks, dtype=jnp.int32)

    def column_table(symmetry):
        return slot_table(symmetry, vir_sym, MAXB)

    gathered = lax.all_gather(amplitudes, "vir", axis=1, tiled=True)
    allowed = (occ_sym[:, None] == k_sym[None, :]).astype(jnp.bfloat16)
    amp_masked = (
        gathered.reshape(occ_blocks, BLK, kblocks, BLK) * allowed[:, None, :, None]
    ).reshape(occ_rows, window)
    shard_rows = integrals.shape[0]
    own_count = shard_rows // BLK
    first_block = lax.axis_index("occ") * own_count
    own_ids = first_block + jnp.arange(own_count, dtype=jnp.int32)
    own_syms = jnp.sum(jnp.where(own_ids[:, None] == block_ids[None, :], k_sym[None, :], 0), axis=1)
    start_sum = jnp.zeros((occ_rows, vir_blocks, BLK), jnp.float32)
    tables_v = jax.vmap(column_table)(own_syms)
    packed_v = jnp.einsum(
        "bmv,brvc->brmc",
        tables_v,
        integrals.reshape(own_count, BLK, vir_blocks, BLK),
        preferred_element_type=jnp.float32,
    )
    packed_v = packed_v.astype(jnp.bfloat16).reshape(shard_rows, MAXB * BLK)
    shard_piece = lax.all_gather(packed_v, "occ", axis=0, tiled=True)
    piece_blocks = shard_piece.shape[0] // BLK

    def one_block(block_index, running_sum):
        row_start = block_index * BLK
        symmetry = jnp.sum(jnp.where(block_ids == row_start // BLK, k_sym, 0))
        chosen = slot_order(symmetry, vir_sym, MAXB)[0]
        amp_cols = lax.dynamic_slice_in_dim(amp_masked, row_start, BLK, 1)
        block_part = lax.dynamic_slice_in_dim(shard_piece, block_index * BLK, BLK, 0)
        product = jnp.dot(amp_cols, block_part, preferred_element_type=jnp.float32)
        return running_sum.at[:, chosen, :].add(product.reshape(occ_rows, MAXB, BLK))

    summed = lax.fori_loop(0, piece_blocks, one_block, start_sum)
    return summed.reshape(occ_rows, col_width).astype(jnp.bfloat16)


def solution(mesh):
    return jax.shard_map(
        per_device,
        mesh=mesh,
        in_specs=(P("occ", "vir"), P("occ", "vir"), P("occ"), P("vir"), P()),
        out_specs=P("occ", "vir"),
        check_vma=False,
    )
```

profile of v0, /device:TPU:1, one launch (start us, length us, event | category | flops | bytes accessed | tf_op | source)
XLA Modules:
  0.0 399.7 jit_solution(3272119504203592197)
XLA Ops:
  15.0 85.2 %all-gather.3.cloned.1.call-done = bf16[768,2048]{0,1:T(8,128)(2,1)} async-done(((bf16[768,32]{0,1:T(8,128)(2,1)}), bf16[768,2048]{0,1:T(8,128)(2,1)}) %all-gather.3.cloned.1.call-update) | async-done | bytes 3145744 | tf_op jit(solution)/shard_map/all_gather | solution.py:37
  100.2 3.2 copy.43
  106.2 43.9 %all-gather.5.cloned.1.call-done = bf16[2048,640]{0,1:T(8,128)(2,1)} async-done(((bf16[256,640]{0,1:T(8,128)(2,1)}), bf16[2048,640]{0,1:T(8,128)(2,1)}) %all-gather.5.cloned.1.call-update) | async-done | bytes 2621456 | tf_op jit(solution)/shard_map/all_gather | solution.py:56
  150.1 3.9 broadcast_in_dim.62
  154.1 225.4 %while.16 = (s32[]{:T(128)}, f32[768,20,128]{2,0,1:T(8,128)}, s32[16]{0:T(128)S(1)}, s32[20]{0:T(128)S(1)}, bf16[768,2048]{1,0:T(8,128)(2,1)}, /*index=5*/bf16[2...) while((s32[]{:T(128)}, f32[768,20,128]{2,0,1:T(8,128)}, ...), condition=%wide.region_6.7_spmd.clone, body=%wide.region_2.6_spmd.clone.sunk | while | flops 126320880 | bytes 12158960 | solution.py:68
  157.1 2.7 fusion.23
  161.7 6.4 %scatter_fusion = f32[768,20,128]{2,0,1:T(8,128)} fusion(f32[768,20,128]{2,0,1:T(8,128)} %get-tuple-element.294, s32[5]{0:T(128)S(1)} %compare_select_fusion.8, f32[5,768,128]{2,1,0:T(8,128)S(1)} %bitcast.27), kind=kCustom, calls=%fused_computation.1.clone.clone.1 | custom fusion | flops 491520 | bytes 5898260 | tf_op jit(solution)/shard_map/while/body/eval_jaxpr/scatter-add | solution.py:66
  171.2 2.7 fusion.23
  175.8 6.4 %scatter_fusion = f32[768,20,128]{2,0,1:T(8,128)} fusion(f32[768,20,128]{2,0,1:T(8,128)} %get-tuple-element.294, s32[5]{0:T(128)S(1)} %compare_select_fusion.8, f32[5,768,128]{2,1,0:T(8,128)S(1)} %bitcast.27), kind=kCustom, calls=%fused_computation.1.clone.clone.1 | custom fusion | flops 491520 | bytes 5898260 | tf_op jit(solution)/shard_map/while/body/eval_jaxpr/scatter-add | solution.py:66
  185.3 2.7 fusion.23
  189.8 6.4 %scatter_fusion = f32[768,20,128]{2,0,1:T(8,128)} fusion(f32[768,20,128]{2,0,1:T(8,128)} %get-tuple-element.294, s32[5]{0:T(128)S(1)} %compare_select_fusion.8, f32[5,768,128]{2,1,0:T(8,128)S(1)} %bitcast.27), kind=kCustom, calls=%fused_computation.1.clone.clone.1 | custom fusion | flops 491520 | bytes 5898260 | tf_op jit(solution)/shard_map/while/body/eval_jaxpr/scatter-add | solution.py:66
  199.3 2.7 fusion.23
  203.9 6.5 %scatter_fusion = f32[768,20,128]{2,0,1:T(8,128)} fusion(f32[768,20,128]{2,0,1:T(8,128)} %get-tuple-element.294, s32[5]{0:T(128)S(1)} %compare_select_fusion.8, f32[5,768,128]{2,1,0:T(8,128)S(1)} %bitcast.27), kind=kCustom, calls=%fused_computation.1.clone.clone.1 | custom fusion | flops 491520 | bytes 5898260 | tf_op jit(solution)/shard_map/while/body/eval_jaxpr/scatter-add | solution.py:66
  218.0 6.5 %scatter_fusion = f32[768,20,128]{2,0,1:T(8,128)} fusion(f32[768,20,128]{2,0,1:T(8,128)} %get-tuple-element.294, s32[5]{0:T(128)S(1)} %compare_select_fusion.8, f32[5,768,128]{2,1,0:T(8,128)S(1)} %bitcast.27), kind=kCustom, calls=%fused_computation.1.clone.clone.1 | custom fusion | flops 491520 | bytes 5898260 | tf_op jit(solution)/shard_map/while/body/eval_jaxpr/scatter-add | solution.py:66
  232.1 6.4 %scatter_fusion = f32[768,20,128]{2,0,1:T(8,128)} fusion(f32[768,20,128]{2,0,1:T(8,128)} %get-tuple-element.294, s32[5]{0:T(128)S(1)} %compare_select_fusion.8, f32[5,768,128]{2,1,0:T(8,128)S(1)} %bitcast.27), kind=kCustom, calls=%fused_computation.1.clone.clone.1 | custom fusion | flops 491520 | bytes 5898260 | tf_op jit(solution)/shard_map/while/body/eval_jaxpr/scatter-add | solution.py:66
  246.2 6.5 %scatter_fusion = f32[768,20,128]{2,0,1:T(8,128)} fusion(f32[768,20,128]{2,0,1:T(8,128)} %get-tuple-element.294, s32[5]{0:T(128)S(1)} %compare_select_fusion.8, f32[5,768,128]{2,1,0:T(8,128)S(1)} %bitcast.27), kind=kCustom, calls=%fused_computation.1.clone.clone.1 | custom fusion | flops 491520 | bytes 5898260 | tf_op jit(solution)/shard_map/while/body/eval_jaxpr/scatter-add | solution.py:66
  260.3 6.5 %scatter_fusion = f32[768,20,128]{2,0,1:T(8,128)} fusion(f32[768,20,128]{2,0,1:T(8,128)} %get-tuple-element.294, s32[5]{0:T(128)S(1)} %compare_select_fusion.8, f32[5,768,128]{2,1,0:T(8,128)S(1)} %bitcast.27), kind=kCustom, calls=%fused_computation.1.clone.clone.1 | custom fusion | flops 491520 | bytes 5898260 | tf_op jit(solution)/shard_map/while/body/eval_jaxpr/scatter-add | solution.py:66
  274.4 6.4 %scatter_fusion = f32[768,20,128]{2,0,1:T(8,128)} fusion(f32[768,20,128]{2,0,1:T(8,128)} %get-tuple-element.294, s32[5]{0:T(128)S(1)} %compare_select_fusion.8, f32[5,768,128]{2,1,0:T(8,128)S(1)} %bitcast.27), kind=kCustom, calls=%fused_computation.1.clone.clone.1 | custom fusion | flops 491520 | bytes 5898260 | tf_op jit(solution)/shard_map/while/body/eval_jaxpr/scatter-add | solution.py:66
  288.5 6.4 %scatter_fusion = f32[768,20,128]{2,0,1:T(8,128)} fusion(f32[768,20,128]{2,0,1:T(8,128)} %get-tuple-element.294, s32[5]{0:T(128)S(1)} %compare_select_fusion.8, f32[5,768,128]{2,1,0:T(8,128)S(1)} %bitcast.27), kind=kCustom, calls=%fused_computation.1.clone.clone.1 | custom fusion | flops 491520 | bytes 5898260 | tf_op jit(solution)/shard_map/while/body/eval_jaxpr/scatter-add | solution.py:66
  298.0 2.7 fusion.23
  302.6 6.4 %scatter_fusion = f32[768,20,128]{2,0,1:T(8,128)} fusion(f32[768,20,128]{2,0,1:T(8,128)} %get-tuple-element.294, s32[5]{0:T(128)S(1)} %compare_select_fusion.8, f32[5,768,128]{2,1,0:T(8,128)S(1)} %bitcast.27), kind=kCustom, calls=%fused_computation.1.clone.clone.1 | custom fusion | flops 491520 | bytes 5898260 | tf_op jit(solution)/shard_map/while/body/eval_jaxpr/scatter-add | solution.py:66
  312.0 2.7 fusion.23
  316.6 6.4 %scatter_fusion = f32[768,20,128]{2,0,1:T(8,128)} fusion(f32[768,20,128]{2,0,1:T(8,128)} %get-tuple-element.294, s32[5]{0:T(128)S(1)} %compare_select_fusion.8, f32[5,768,128]{2,1,0:T(8,128)S(1)} %bitcast.27), kind=kCustom, calls=%fused_computation.1.clone.clone.1 | custom fusion | flops 491520 | bytes 5898260 | tf_op jit(solution)/shard_map/while/body/eval_jaxpr/scatter-add | solution.py:66
  326.1 2.7 fusion.23
  330.7 6.4 %scatter_fusion = f32[768,20,128]{2,0,1:T(8,128)} fusion(f32[768,20,128]{2,0,1:T(8,128)} %get-tuple-element.294, s32[5]{0:T(128)S(1)} %compare_select_fusion.8, f32[5,768,128]{2,1,0:T(8,128)S(1)} %bitcast.27), kind=kCustom, calls=%fused_computation.1.clone.clone.1 | custom fusion | flops 491520 | bytes 5898260 | tf_op jit(solution)/shard_map/while/body/eval_jaxpr/scatter-add | solution.py:66
  340.2 2.7 fusion.23
  344.8 6.5 %scatter_fusion = f32[768,20,128]{2,0,1:T(8,128)} fusion(f32[768,20,128]{2,0,1:T(8,128)} %get-tuple-element.294, s32[5]{0:T(128)S(1)} %compare_select_fusion.8, f32[5,768,128]{2,1,0:T(8,128)S(1)} %bitcast.27), kind=kCustom, calls=%fused_computation.1.clone.clone.1 | custom fusion | flops 491520 | bytes 5898260 | tf_op jit(solution)/shard_map/while/body/eval_jaxpr/scatter-add | solution.py:66
  354.3 2.7 fusion.23
  358.9 6.5 %scatter_fusion = f32[768,20,128]{2,0,1:T(8,128)} fusion(f32[768,20,128]{2,0,1:T(8,128)} %get-tuple-element.294, s32[5]{0:T(128)S(1)} %compare_select_fusion.8, f32[5,768,128]{2,1,0:T(8,128)S(1)} %bitcast.27), kind=kCustom, calls=%fused_computation.1.clone.clone.1 | custom fusion | flops 491520 | bytes 5898260 | tf_op jit(solution)/shard_map/while/body/eval_jaxpr/scatter-add | solution.py:66
  373.0 6.4 %scatter_fusion = f32[768,20,128]{2,0,1:T(8,128)} fusion(f32[768,20,128]{2,0,1:T(8,128)} %get-tuple-element.294, s32[5]{0:T(128)S(1)} %compare_select_fusion.8, f32[5,768,128]{2,1,0:T(8,128)S(1)} %bitcast.27), kind=kCustom, calls=%fused_computation.1.clone.clone.1 | custom fusion | flops 491520 | bytes 5898260 | tf_op jit(solution)/shard_map/while/body/eval_jaxpr/scatter-add | solution.py:66
  379.4 7.2 %copy.51 = bf16[768,20,128]{0,2,1:T(8,128)(2,1)} copy(f32[768,20,128]{2,0,1:T(8,128)} %get-tuple-element.185) | data formatting | bytes 11796480 | tf_op jit(solution)/shard_map/while | solution.py:68
  386.6 6.3 %copy.52 = bf16[768,2560]{1,0:T(8,128)(2,1)} copy(bf16[768,2560]{0,1:T(8,128)(2,1)} %bitcast.29) | data formatting | bytes 7864320 | tf_op jit(solution)/shard_map/convert_element_type | solution.py:69
  (134 shorter events, 108.8 us)
Async XLA Ops:
  6.5 93.6 %all-gather.3.cloned.1.call-start = ((), (), s32[]{:S(2)}) async-start(), calls=%async_computation | async-start | bytes 3194880 | tf_op jit(solution)/shard_map/all_gather | solution.py:37
  7.3 142.9 %all-gather.5.cloned.1.call-start = ((), (), s32[]{:S(2)}) async-start(), calls=%async_computation.1 | async-start | bytes 2949120 | tf_op jit(solution)/shard_map/all_gather | solution.py:56
  10.9 4.0 copy-start
  10.9 4.0 %copy-start.1 = (s32[16]{0:T(128)S(1)}, s32[16]{0:T(128)}, u32[]{:S(2)}) copy-start(s32[16]{0:T(128)} %param.11) | copy-start | bytes 196
  106.2 47.8 %copy-start.2 = (s32[20]{0:T(128)S(1)}, s32[20]{0:T(128)}, u32[]{:S(2)}) copy-start(s32[20]{0:T(128)} %param.10) | copy-start | bytes 244
Sparse Core Ops, SparseCore 0:
  10.7 89.4 all-gather.2
  102.2 47.8 all-gather.4
where the time goes:
time: 405 us; the launch traced here: 400 us
  other arithmetic  157 us (39%)
  waiting for transfers between devices  130 us (32%)
  local copies, waits for them, and re-layouts  56 us (14%)
  matrix products  43.5 us (11%)
  between operations  13.5 us (3%)
    scatter-add x16, other arithmetic, one_block(): running_sum.at[:, chosen, :].add(product.reshape(occ_rows, MAXB, BLK))  103 us
    all_gather x1, waiting for transfers between devices, per_device(): gathered = lax.all_gather(amplitudes, 'vir', axis=1, tiled=True)  85.2 us
    all_gather x1, waiting for transfers between devices, per_device(): shard_piece = lax.all_gather(packed_v, 'occ', axis=0, tiled=True)  43.9 us
    dot_general x16, matrix products, one_block(): product = jnp.dot(amp_cols, block_part, preferred_element_type=jnp.float32)  43.1 us
    reshape x16, local copies, waits for them, and re-layouts, one_block(): product.reshape(occ_rows, MAXB, BLK)  30.2 us
    sort x17, other arithmetic, slot_order(): chosen = jnp.argsort(ranking)[:slot_bound]  27.5 us
    select_n x17, other arithmetic, slot_order(): ranking = jnp.where(matching, positions, positions + label_count)  11.5 us
    reduce_sum x16, other arithmetic, one_block(): symmetry = jnp.sum(jnp.where(block_ids == row_start // BLK, k_sym, 0))  11.1 us
  transfers between devices with their start and end apart: 2, of which 2 were waited for; matrix products, arithmetic and copies ran while one was open for 3% of the time, Pallas kernels for 0%

commit v1 on v0

v1 whole, which is shorter than its diff:
```python
import jax
import jax.numpy as jnp
from jax import lax
from jax.experimental import pallas as pl
from jax.experimental.pallas import tpu as pltpu
from jax.sharding import PartitionSpec as P

BLK = 128
MAXO = 2
MAXB = 5
NZ, NY, NX = 8, 8, 4
PIECES = 4
MESH = pl.DeviceIdType.MESH


def ladder_kernel(occ_s, vir_s, k_s, a_hbm, v_hbm, out_ref, a_in, v_in, ag, vbuf, amask, acc,
                  in_sem, vsend, vrecv, xsend, xrecv, ysend, yrecv, csend, crecv):
    occ_rows = out_ref.shape[0]
    occ_blocks = occ_rows // BLK
    vir_blocks = vir_s.shape[0]
    width = MAXB * BLK
    z = lax.axis_index("occ")
    v = lax.axis_index("vir")
    y = lax.div(v, 2 * NX)
    x = lax.rem(lax.div(v, 2), NX)
    c = lax.rem(v, 2)

    def vir_at(yy, xx, cc):
        return (yy * NX + xx) * 2 + cc

    def ring(value, step, size):
        return lax.rem(value + step + size, size)

    z_next, z_prev = (ring(z, 1, NZ), v), (ring(z, -1, NZ), v)
    y_next, y_prev = (z, vir_at(ring(y, 1, NY), x, c)), (z, vir_at(ring(y, -1, NY), x, c))
    x_far = {step: (z, vir_at(y, ring(x, step, NX), c)) for step in (1, 3, 2)}
    twin = (z, vir_at(y, x, 1 - c))
    partners = [z_next, z_prev, y_next, y_prev, twin] + list(x_far.values())

    barrier = pltpu.get_barrier_semaphore()
    for partner in partners:
        pl.semaphore_signal(barrier, inc=1, device_id=partner, device_id_type=MESH)
    load_v = pltpu.make_async_copy(v_hbm, v_in, in_sem.at[0])
    load_a = pltpu.make_async_copy(a_hbm, a_in, in_sem.at[1])
    load_v.start()
    load_a.start()

    def picks(labels, count, symmetry, slots):
        chosen, taken = [], jnp.int32(0)
        for j in range(count):
            match = jnp.where(labels[j] == symmetry, 1, 0)
            chosen.append([match * jnp.where(taken == t, 1, 0) == 1 for t in range(slots)])
            taken = taken + match
        return chosen

    def pick(blocks, chosen, t):
        value = blocks[t]
        for j in range(t + 1, len(blocks)):
            value = lax.select(chosen[j][t], blocks[j], value)
        return value

    own_picks = [picks(vir_s, vir_blocks, k_s[2 * z + half], MAXB) for half in range(2)]
    row_picks = picks(occ_s, occ_blocks, k_s[lax.div(v, 4)], MAXO)

    load_a.wait()
    for t in range(MAXO):
        blocks = [a_in[:, i * BLK:(i + 1) * BLK] for i in range(occ_blocks)]
        ag[c, y, x, :, t * BLK:(t + 1) * BLK] = pick(blocks, row_picks, t)
    load_v.wait()
    for half in range(2):
        for strip in range(0, BLK, 32):
            span = slice(half * BLK + strip, half * BLK + strip + 32)
            blocks = [v_in[span, j * BLK:(j + 1) * BLK] for j in range(vir_blocks)]
            for t in range(MAXB):
                vbuf[0, span, t * BLK:(t + 1) * BLK] = pick(blocks, own_picks[half], t)

    pl.semaphore_wait(barrier, len(partners))

    rows = 2 * BLK // PIECES
    piece_order = ((0, 1, 2, 3), (2, 3, 0, 1))
    slots = ((0, 1, 2, 3, 7), (0, 4, 5, 6, 7))

    def v_copy(way, index):
        step, piece = index // PIECES, piece_order[way][index % PIECES]
        span = slice(piece * rows, (piece + 1) * rows)
        return pltpu.make_async_remote_copy(
            src_ref=vbuf.at[slots[way][step], span, :], dst_ref=vbuf.at[slots[way][step + 1], span, :],
            send_sem=vsend.at[way, index], recv_sem=vrecv.at[way, index],
            device_id=(z_next, z_prev)[way], device_id_type=MESH)

    v_count = 3 * PIECES + PIECES // 2
    v_copies = [[v_copy(way, index) for index in range(v_count)] for way in range(2)]

    def x_copy(step):
        return pltpu.make_async_remote_copy(
            src_ref=ag.at[c, y, x], dst_ref=ag.at[c, y, x], send_sem=xsend.at[step - 1], recv_sem=xrecv.at[step - 1],
            device_id=x_far[step], device_id_type=MESH)

    def y_copy(way, step):
        group = ring(y, -step if way == 0 else step, NY)
        return pltpu.make_async_remote_copy(
            src_ref=ag.at[c, group], dst_ref=ag.at[c, group], send_sem=ysend.at[way, step], recv_sem=yrecv.at[way, step],
            device_id=(y_next, y_prev)[way], device_id_type=MESH)

    def c_copy(step):
        group = ring(y, -step, NY)
        return pltpu.make_async_remote_copy(
            src_ref=ag.at[c, group], dst_ref=ag.at[c, group], send_sem=csend.at[step], recv_sem=crecv.at[step],
            device_id=twin, device_id_type=MESH)

    x_copies = [x_copy(step) for step in (1, 3, 2)]
    y_copies = [[y_copy(0, step) for step in range(4)], [y_copy(1, step) for step in range(3)]]
    c_copies = [c_copy(step) for step in range(NY)]

    for piece in range(PIECES):
        for way in range(2):
            v_copies[way][piece].start()
        if piece == 0:
            for copy in x_copies:
                copy.start()

    def v_pass(index):
        for way in range(2):
            v_copies[way][index].wait_recv()
            if index + PIECES < v_count:
                v_copies[way][index + PIECES].start()

    def y_pass(step):
        for way in range(2):
            if step <= len(y_copies[way]):
                y_copies[way][step - 1].wait_recv()
                if step < len(y_copies[way]):
                    y_copies[way][step].start()
                c_copies[step if way == 0 else NY - step].start()

    def build(group):
        for half in range(2):
            kb = group * 2 + half
            stacked = jnp.concatenate([ag[cc, group, 2 * half + xx] for xx in range(2) for cc in range(2)], axis=0)
            turned = [stacked[:, t * BLK:(t + 1) * BLK].T.astype(jnp.float32) for t in range(MAXO)]
            symmetry = k_s[kb]
            for i in range(occ_blocks):
                first = jnp.int32(0)
                for other in range(i):
                    first = first + jnp.where(occ_s[other] == occ_s[i], 1, 0)
                match = jnp.where(occ_s[i] == symmetry, 1, 0)
                scale = [(match * jnp.where(first == t, 1, 0)).astype(jnp.float32) for t in range(MAXO)]
                chosen = turned[0] * scale[0] + turned[1] * scale[1]
                amask[i * BLK:(i + 1) * BLK, pl.ds(pl.multiple_of(kb * BLK, BLK), BLK)] = chosen.astype(jnp.bfloat16)

    def product(slot, distance):
        origin = ring(z, -distance, NZ)
        left = amask[:, pl.ds(pl.multiple_of(origin * (2 * BLK), 2 * BLK), 2 * BLK)]
        return jnp.dot(left, vbuf[slot], preferred_element_type=jnp.float32)

    for copy in x_copies:
        copy.wait_recv()
    y_copies[0][0].start()
    y_copies[1][0].start()
    c_copies[0].start()
    v_pass(0)
    v_pass(1)
    y_pass(1)
    v_pass(2)
    v_pass(3)
    y_pass(2)
    v_pass(4)
    y_pass(3)
    v_pass(5)
    v_pass(6)
    y_pass(4)
    for copy in c_copies:
        copy.wait_recv()
    v_pass(7)

    @pl.loop(0, NY)
    def _(group):
        build(group)

    v_pass(8)
    acc[...] = product(0, 0)
    acc[...] += product(1, 1)
    v_pass(9)
    acc[...] += product(4, -1)
    acc[...] += product(2, 2)
    v_pass(10)
    acc[...] += product(5, -2)
    v_pass(11)
    acc[...] += product(3, 3)
    acc[...] += product(6, -3)
    v_pass(12)
    v_pass(13)
    out_ref[...] = (acc[...] + product(7, 4)).astype(out_ref.dtype)

    for copy in v_copies[0] + v_copies[1] + x_copies + y_copies[0] + y_copies[1] + c_copies:
        copy.wait_send()


def expand_kernel(occ_s, vir_s, packed, out_ref):
    symmetry = occ_s[pl.program_id(0)]
    taken = jnp.int32(0)
    for j in range(vir_s.shape[0]):
        match = vir_s[j] == symmetry
        slot = pl.multiple_of(jnp.minimum(taken, MAXB - 1) * BLK, BLK)
        block = packed[:, pl.ds(slot, BLK)]
        out_ref[:, j * BLK:(j + 1) * BLK] = lax.select(match, block, jnp.zeros_like(block))
        taken = taken + jnp.where(match, 1, 0)


def per_device(amplitudes, integrals, occ_sym, vir_sym, k_sym):
    occ_rows, part = amplitudes.shape
    depth, columns = integrals.shape
    width = MAXB * BLK
    bf16 = jnp.bfloat16
    smem = pl.BlockSpec(memory_space=pltpu.SMEM)
    anywhere = pl.BlockSpec(memory_space=pl.ANY)
    v_count = 3 * PIECES + PIECES // 2
    dma = pltpu.SemaphoreType.DMA
    packed = pl.pallas_call(
        ladder_kernel,
        out_shape=jax.ShapeDtypeStruct((occ_rows, width), bf16),
        in_specs=[smem, smem, smem, anywhere, anywhere],
        out_specs=pl.BlockSpec(memory_space=pltpu.VMEM),
        scratch_shapes=[
            pltpu.VMEM((part, occ_rows), bf16),
            pltpu.VMEM((depth, columns), bf16),
            pltpu.VMEM((2, NY, NX, part, MAXO * BLK), bf16),
            pltpu.VMEM((NZ, depth, width), bf16),
            pltpu.VMEM((occ_rows, NZ * depth), bf16),
            pltpu.VMEM((occ_rows, width), jnp.float32),
            dma((2,)),
            dma((2, v_count)), dma((2, v_count)),
            dma((3,)), dma((3,)),
            dma((2, 4)), dma((2, 4)),
            dma((NY,)), dma((NY,)),
        ],
        compiler_params=pltpu.CompilerParams(collective_id=0, has_side_effects=True),
        name="ladder_ring",
    )(occ_sym, vir_sym, k_sym, amplitudes.T, integrals)
    return pl.pallas_call(
        expand_kernel,
        grid=(occ_rows // BLK,),
        out_shape=jax.ShapeDtypeStruct((occ_rows, columns), bf16),
        in_specs=[smem, smem, pl.BlockSpec((BLK, width), lambda i: (i, 0))],
        out_specs=pl.BlockSpec((BLK, columns), lambda i: (i, 0)),
        name="expand",
    )(occ_sym, vir_sym, packed)


def solution(mesh):
    return jax.shard_map(
        per_device,
        mesh=mesh,
        in_specs=(P("occ", "vir"), P("occ", "vir"), P("occ"), P("vir"), P()),
        out_specs=P("occ", "vir"),
        check_vma=False,
    )
```

time: 405 us -> 50.4 us (0.12); the launches traced: 400 us -> 50.2 us
  other arithmetic: 157 us -> 0 us
  waiting for transfers between devices: 130 us -> 0 us
  local copies, waits for them, and re-layouts: 56 us -> 0 us
  Pallas kernels: 0 us -> 50.2 us
  matrix products: 43.5 us -> 0 us
  between operations: 13.5 us -> 0.01 us
    all_gather x2 -> x0, waiting for transfers between devices: 129 us -> none  [the longest x1 85.2 us: per_device(): gathered = lax.all_gather(amplitudes, 'vir', axis=1, tiled=True)]
    scatter-add x16 -> x0, other arithmetic: 103 us -> none  [one_block(): running_sum.at[:, chosen, :].add(product.reshape(occ_rows, MAXB, BLK))]
    pallas_call x0 -> x2, Pallas kernels: none -> 50.2 us  [the longest x1 44.9 us: per_device(): pl.pallas_call(ladder_kernel, out_shape=jax.ShapeDtypeStruct((occ_rows, w...]
    dot_general x17 -> x0, matrix products: 43.5 us -> none  [the longest x16 43.1 us: one_block(): product = jnp.dot(amp_cols, block_part, preferred_element_type=jnp.float32)]
    reshape x18 -> x0, local copies, waits for them, and re-layouts: 33.6 us -> none  [the longest x16 30.2 us: one_block(): product.reshape(occ_rows, MAXB, BLK)]
    sort x17 -> x0, other arithmetic: 27.5 us -> none  [slot_order(): chosen = jnp.argsort(ranking)[:slot_bound]]
    reduce_sum x17 -> x0, other arithmetic: 11.9 us -> none  [the longest x16 11.1 us: one_block(): symmetry = jnp.sum(jnp.where(block_ids == row_start // BLK, k_sym, 0))]
    select_n x33 -> x0, other arithmetic: 11.5 us -> none  [the longest x17 11.5 us: slot_order(): ranking = jnp.where(matching, positions, positions + label_count)]
  transfers between devices with their start and end apart: 2 -> 0, of which waited for: 2 -> 0; matrix products, arithmetic and copies ran while one was open for 3% -> 0% of each run, Pallas kernels for 0% -> 0%
where the time goes in v1:
time: 50.4 us; the launch traced here: 50.2 us
  Pallas kernels  50.2 us (100%)
    pallas_call x1, Pallas kernels, per_device(): pl.pallas_call(ladder_kernel, out_shape=jax.ShapeDtypeStruct((occ_rows, w...  44.9 us
    pallas_call x1, Pallas kernels, per_device(): pl.pallas_call(expand_kernel, grid=(occ_rows // BLK,), out_shape=jax.Shap...  5.28 us

profile of v1, /device:TPU:1, one launch (start us, length us, event | category | flops | bytes accessed | tf_op | source)
XLA Modules:
  0.0 50.2 jit_solution(10330032521997633572)
XLA Ops:
  0.0 44.9 %ladder_ring.1.packed = bf16[768,640]{1,0:T(8,128)(2,1)} custom-call(s32[6]{0:T(128)} %occ_s.3, s32[20]{0:T(128)} %vir_s.3, s32[16]{0:T(128)} %k_s.1, bf16[32,768]{1,0:T(8,128)(2,1)} %bitcast.1, bf16[256,2560]{1,0:T(8,128)(2,1)} %v_hbm.1), custom_call_target="tpu_custom_call" | custom-call | tf_op jit(solution)/shard_map/ladder_ring/pallas_call | solution.py:219
  44.9 5.3 %expand.1 = bf16[768,2560]{1,0:T(8,128)(2,1)} custom-call(s32[6]{0:T(128)} %occ_s.3, s32[20]{0:T(128)} %vir_s.3, bf16[768,640]{1,0:T(8,128)(2,1)} %ladder_ring.1.packed), custom_call_target="tpu_custom_call" | custom-call | tf_op jit(solution)/shard_map/expand/pallas_call | solution.py:240

commit v2 on v1

--- a/solution.py
+++ b/solution.py
@@ -13,12 +13,11 @@
 MESH = pl.DeviceIdType.MESH
 
 
-def ladder_kernel(occ_s, vir_s, k_s, a_hbm, v_hbm, out_ref, a_in, v_in, ag, vbuf, amask, acc,
+def ladder_kernel(occ_hbm, vir_hbm, k_hbm, a_hbm, v_hbm, out_ref, occ_s, vir_s, k_s, a_in, v_in, ag, vbuf, amask, acc,
                   in_sem, vsend, vrecv, xsend, xrecv, ysend, yrecv, csend, crecv):
     occ_rows = out_ref.shape[0]
     occ_blocks = occ_rows // BLK
     vir_blocks = vir_s.shape[0]
-    width = MAXB * BLK
     z = lax.axis_index("occ")
     v = lax.axis_index("vir")
     y = lax.div(v, 2 * NX)
@@ -37,13 +36,21 @@
     twin = (z, vir_at(y, x, 1 - c))
     partners = [z_next, z_prev, y_next, y_prev, twin] + list(x_far.values())
 
+    rows = 2 * BLK // PIECES
     barrier = pltpu.get_barrier_semaphore()
     for partner in partners:
         pl.semaphore_signal(barrier, inc=1, device_id=partner, device_id_type=MESH)
-    load_v = pltpu.make_async_copy(v_hbm, v_in, in_sem.at[0])
-    load_a = pltpu.make_async_copy(a_hbm, a_in, in_sem.at[1])
-    load_v.start()
-    load_a.start()
+    loads = [pltpu.make_async_copy(source, target, in_sem.at[index])
+             for index, (source, target) in enumerate([(k_hbm, k_s), (vir_hbm, vir_s), (occ_hbm, occ_s), (a_hbm, a_in)])]
+    v_loads = [pltpu.make_async_copy(v_hbm.at[piece * rows:(piece + 1) * rows], v_in.at[piece * rows:(piece + 1) * rows], in_sem.at[4 + piece])
+               for piece in range(PIECES)]
+    for load in loads[:3]:
+        load.start()
+    for piece in (0, 2, 1, 3):
+        v_loads[piece].start()
+    loads[3].start()
+    for load in loads[:3]:
+        load.wait()
 
     def picks(labels, count, symmetry, slots):
         chosen, taken = [], jnp.int32(0)
@@ -62,21 +69,23 @@
     own_picks = [picks(vir_s, vir_blocks, k_s[2 * z + half], MAXB) for half in range(2)]
     row_picks = picks(occ_s, occ_blocks, k_s[lax.div(v, 4)], MAXO)
 
-    load_a.wait()
+    def pack(piece):
+        v_loads[piece].wait()
+        for strip in range(piece * rows, (piece + 1) * rows, 32):
+            span = slice(strip, strip + 32)
+            blocks = [v_in[span, j * BLK:(j + 1) * BLK] for j in range(vir_blocks)]
+            for t in range(MAXB):
+                vbuf[0, span, t * BLK:(t + 1) * BLK] = pick(blocks, own_picks[strip // BLK], t)
+
+    for piece in (0, 2, 1, 3):
+        pack(piece)
+    loads[3].wait()
     for t in range(MAXO):
         blocks = [a_in[:, i * BLK:(i + 1) * BLK] for i in range(occ_blocks)]
         ag[c, y, x, :, t * BLK:(t + 1) * BLK] = pick(blocks, row_picks, t)
-    load_v.wait()
-    for half in range(2):
-        for strip in range(0, BLK, 32):
-            span = slice(half * BLK + strip, half * BLK + strip + 32)
-            blocks = [v_in[span, j * BLK:(j + 1) * BLK] for j in range(vir_blocks)]
-            for t in range(MAXB):
-                vbuf[0, span, t * BLK:(t + 1) * BLK] = pick(blocks, own_picks[half], t)
 
     pl.semaphore_wait(barrier, len(partners))
 
-    rows = 2 * BLK // PIECES
     piece_order = ((0, 1, 2, 3), (2, 3, 0, 1))
     slots = ((0, 1, 2, 3, 7), (0, 4, 5, 6, 7))
 
@@ -196,15 +205,25 @@
         copy.wait_send()
 
 
-def expand_kernel(occ_s, vir_s, packed, out_ref):
-    symmetry = occ_s[pl.program_id(0)]
-    taken = jnp.int32(0)
-    for j in range(vir_s.shape[0]):
-        match = vir_s[j] == symmetry
-        slot = pl.multiple_of(jnp.minimum(taken, MAXB - 1) * BLK, BLK)
-        block = packed[:, pl.ds(slot, BLK)]
-        out_ref[:, j * BLK:(j + 1) * BLK] = lax.select(match, block, jnp.zeros_like(block))
-        taken = taken + jnp.where(match, 1, 0)
+def expand_kernel(occ_s, vir_s, packed, out_hbm, full, sems):
+    copies = []
+    for i in range(occ_s.shape[0]):
+        span = slice(i * BLK, (i + 1) * BLK)
+        taken = jnp.int32(0)
+        for j in range(vir_s.shape[0]):
+            match = vir_s[j] == occ_s[i]
+            slot = pl.multiple_of(jnp.minimum(taken, MAXB - 1) * BLK, BLK)
+            block = packed[span, pl.ds(slot, BLK)]
+            full[span, j * BLK:(j + 1) * BLK] = lax.select(match, block, jnp.zeros_like(block))
+            taken = taken + jnp.where(match, 1, 0)
+        copies.append(pltpu.make_async_copy(full.at[span], out_hbm.at[span], sems.at[i]))
+        copies[-1].start()
+    for copy in copies:
+        copy.wait()
+
+
+def in_hbm(array):
+    return pltpu.with_memory_space_constraint(array, pltpu.HBM)
 
 
 def per_device(amplitudes, integrals, occ_sym, vir_sym, k_sym):
@@ -213,36 +232,42 @@
     width = MAXB * BLK
     bf16 = jnp.bfloat16
     smem = pl.BlockSpec(memory_space=pltpu.SMEM)
-    anywhere = pl.BlockSpec(memory_space=pl.ANY)
+    vmem = pl.BlockSpec(memory_space=pltpu.VMEM)
+    hbm = pl.BlockSpec(memory_space=pltpu.HBM)
     v_count = 3 * PIECES + PIECES // 2
     dma = pltpu.SemaphoreType.DMA
+    occ_sym, vir_sym, k_sym = in_hbm(occ_sym), in_hbm(vir_sym), in_hbm(k_sym)
     packed = pl.pallas_call(
         ladder_kernel,
-        out_shape=jax.ShapeDtypeStruct((occ_rows, width), bf16),
-        in_specs=[smem, smem, smem, anywhere, anywhere],
-        out_specs=pl.BlockSpec(memory_space=pltpu.VMEM),
+        out_shape=pltpu.VMEM((occ_rows, width), bf16),
+        in_specs=[hbm] * 5,
+        out_specs=vmem,
         scratch_shapes=[
+            pltpu.SMEM(occ_sym.shape, jnp.int32),
+            pltpu.SMEM(vir_sym.shape, jnp.int32),
+            pltpu.SMEM(k_sym.shape, jnp.int32),
             pltpu.VMEM((part, occ_rows), bf16),
             pltpu.VMEM((depth, columns), bf16),
             pltpu.VMEM((2, NY, NX, part, MAXO * BLK), bf16),
             pltpu.VMEM((NZ, depth, width), bf16),
             pltpu.VMEM((occ_rows, NZ * depth), bf16),
             pltpu.VMEM((occ_rows, width), jnp.float32),
-            dma((2,)),
+            dma((4 + PIECES,)),
             dma((2, v_count)), dma((2, v_count)),
             dma((3,)), dma((3,)),
             dma((2, 4)), dma((2, 4)),
             dma((NY,)), dma((NY,)),
         ],
-        compiler_params=pltpu.CompilerParams(collective_id=0, has_side_effects=True),
+        compiler_params=pltpu.CompilerParams(collective_id=0, has_side_effects=True, vmem_limit_bytes=24 << 20),
         name="ladder_ring",
-    )(occ_sym, vir_sym, k_sym, amplitudes.T, integrals)
+    )(occ_sym, vir_sym, k_sym, in_hbm(amplitudes.T), in_hbm(integrals))
     return pl.pallas_call(
         expand_kernel,
-        grid=(occ_rows // BLK,),
         out_shape=jax.ShapeDtypeStruct((occ_rows, columns), bf16),
-        in_specs=[smem, smem, pl.BlockSpec((BLK, width), lambda i: (i, 0))],
-        out_specs=pl.BlockSpec((BLK, columns), lambda i: (i, 0)),
+        in_specs=[smem, smem, vmem],
+        out_specs=hbm,
+        scratch_shapes=[pltpu.VMEM((occ_rows, columns), bf16), dma((occ_rows // BLK,))],
+        compiler_params=pltpu.CompilerParams(vmem_limit_bytes=24 << 20),
         name="expand",
     )(occ_sym, vir_sym, packed)
 

time: 50.4 us -> 46.1 us (0.915)
  Pallas kernels: 50.2 us -> 46 us
    pallas_call x2, Pallas kernels: 50.2 us -> 46 us  [the longest x1 43.1 us: per_device(): pl.pallas_call(ladder_kernel, out_shape=pltpu.VMEM((occ_rows, width), bf1...]
where the time goes in v2:
time: 46.1 us; the launch traced here: 46 us
  Pallas kernels  46 us (100%)
    pallas_call x1, Pallas kernels, per_device(): pl.pallas_call(ladder_kernel, out_shape=pltpu.VMEM((occ_rows, width), bf1...  43.1 us
    pallas_call x1, Pallas kernels, per_device(): pl.pallas_call(expand_kernel, out_shape=jax.ShapeDtypeStruct((occ_rows, c...  2.82 us

profile of v2, /device:TPU:1, one launch (start us, length us, event | category | flops | bytes accessed | tf_op | source)
XLA Modules:
  0.0 46.0 jit_solution(17967490129311728505)
XLA Ops:
  0.0 43.1 %ladder_ring.1.packed = bf16[768,640]{1,0:T(8,128)(2,1)S(1)} custom-call(s32[6]{0:T(128)} %occ_s.1, s32[20]{0:T(128)} %vir_s.1, s32[16]{0:T(128)} %k_hbm.1, bf16[32,768]{1,0:T(8,128)(2,1)} %bitcast.1, bf16[256,2560]{1,0:T(8,128)(2,1)} %v_hbm.1), custom_call_target="tpu_custom_call" | custom-call | tf_op jit(solution)/shard_map/ladder_ring/pallas_call | solution.py:240
  43.2 2.8 %expand.1 = bf16[768,2560]{1,0:T(8,128)(2,1)} custom-call(s32[6]{0:T(128)} %occ_s.1, s32[20]{0:T(128)} %vir_s.1, bf16[768,640]{1,0:T(8,128)(2,1)S(1)} %ladder_ring.1.packed), custom_call_target="tpu_custom_call" | custom-call | tf_op jit(solution)/shard_map/expand/pallas_call | solution.py:264

commit v3 on v2

v3 whole, which is shorter than its diff:
```python
import jax
import jax.numpy as jnp
from jax import lax
from jax.experimental import pallas as pl
from jax.experimental.pallas import tpu as pltpu
from jax.sharding import PartitionSpec as P

BLK = 128
MAXO = 2
MAXB = 5
NZ, NY, NX = 8, 8, 4
PIECES = 4
MESH = pl.DeviceIdType.MESH


def ladder_kernel(occ_hbm, vir_hbm, k_hbm, a_hbm, v_hbm, acc, a_last, v_last, occ_s, vir_s, k_s, a_in, v_in, ag, vbuf, amask, unit,
                  in_sem, vsend, vrecv, xsend, xrecv, ysend, yrecv, csend, crecv):
    occ_rows = acc.shape[0]
    occ_blocks = occ_rows // BLK
    depth = v_hbm.shape[0]
    vir_blocks = vir_s.shape[0]
    z = lax.axis_index("occ")
    v = lax.axis_index("vir")
    y = lax.div(v, 2 * NX)
    x = lax.rem(lax.div(v, 2), NX)
    c = lax.rem(v, 2)

    def vir_at(yy, xx, cc):
        return (yy * NX + xx) * 2 + cc

    def ring(value, step, size):
        return lax.rem(value + step + size, size)

    z_next, z_prev = (ring(z, 1, NZ), v), (ring(z, -1, NZ), v)
    y_next, y_prev = (z, vir_at(ring(y, 1, NY), x, c)), (z, vir_at(ring(y, -1, NY), x, c))
    x_far = {step: (z, vir_at(y, ring(x, step, NX), c)) for step in (1, 3, 2)}
    twin = (z, vir_at(y, x, 1 - c))
    partners = [z_next, z_prev, y_next, y_prev, twin] + list(x_far.values())

    rows = 2 * BLK // PIECES
    barrier = pltpu.get_barrier_semaphore()
    for partner in partners:
        pl.semaphore_signal(barrier, inc=1, device_id=partner, device_id_type=MESH)
    loads = [pltpu.make_async_copy(source, target, in_sem.at[index])
             for index, (source, target) in enumerate([(k_hbm, k_s), (vir_hbm, vir_s), (occ_hbm, occ_s), (a_hbm, a_in)])]
    v_loads = [pltpu.make_async_copy(v_hbm.at[piece * rows:(piece + 1) * rows], v_in.at[piece * rows:(piece + 1) * rows], in_sem.at[4 + piece])
               for piece in range(PIECES)]
    for load in loads:
        load.start()
    for piece in (0, 2, 1, 3):
        v_loads[piece].start()
    for load in loads[:3]:
        load.wait()

    def picks(labels, count, symmetry, slots):
        chosen, place = [], jnp.int32(1)
        for j in range(count):
            match = labels[j] == symmetry
            code = jnp.where(match, place, 0)
            chosen.append([code == 1 << t for t in range(slots)])
            place = jnp.where(match, 2 * place, place)
        return chosen

    def pick(blocks, chosen, t):
        value = blocks[t]
        for j in range(t + 1, len(blocks)):
            value = lax.select(chosen[j][t], blocks[j], value)
        return value

    own_picks = [picks(vir_s, vir_blocks, k_s[2 * z + half], MAXB) for half in range(2)]
    row_picks = picks(occ_s, occ_blocks, k_s[lax.div(v, 4)], MAXO)

    def pack(piece):
        v_loads[piece].wait()
        for strip in range(piece * rows, (piece + 1) * rows, 32):
            span = slice(strip, strip + 32)
            blocks = [v_in[span, j * BLK:(j + 1) * BLK] for j in range(vir_blocks)]
            for t in range(MAXB):
                vbuf[span, t * BLK:(t + 1) * BLK] = pick(blocks, own_picks[strip // BLK], t)

    pack(0)
    pack(2)
    pl.semaphore_wait(barrier, len(partners))

    piece_order = ((0, 1, 2, 3), (2, 3, 0, 1))
    slots = ((0, 1, 3, 5, 7), (0, 2, 4, 6, 7))

    def v_copy(way, index):
        step, piece = index // PIECES, piece_order[way][index % PIECES]
        source, target = [slots[way][step + ahead] * depth + piece * rows for ahead in range(2)]
        return pltpu.make_async_remote_copy(
            src_ref=vbuf.at[source:source + rows], dst_ref=vbuf.at[target:target + rows],
            send_sem=vsend.at[way, index], recv_sem=vrecv.at[way, index],
            device_id=(z_next, z_prev)[way], device_id_type=MESH)

    v_counts = (3 * PIECES + PIECES // 2, 4 * PIECES)
    v_copies = [[v_copy(way, index) for index in range(v_counts[way])] for way in range(2)]

    def x_copy(step):
        return pltpu.make_async_remote_copy(
            src_ref=ag.at[c, y, x], dst_ref=ag.at[c, y, x], send_sem=xsend.at[step - 1], recv_sem=xrecv.at[step - 1],
            device_id=x_far[step], device_id_type=MESH)

    def y_copy(way, step):
        group = ring(y, -step if way == 0 else step, NY)
        return pltpu.make_async_remote_copy(
            src_ref=ag.at[c, group], dst_ref=ag.at[c, group], send_sem=ysend.at[way, step], recv_sem=yrecv.at[way, step],
            device_id=(y_next, y_prev)[way], device_id_type=MESH)

    def c_copy(step):
        group = ring(y, -step, NY)
        return pltpu.make_async_remote_copy(
            src_ref=ag.at[c, group], dst_ref=ag.at[c, group], send_sem=csend.at[step], recv_sem=crecv.at[step],
            device_id=twin, device_id_type=MESH)

    x_copies = [x_copy(step) for step in (1, 3, 2)]
    y_copies = [[y_copy(0, step) for step in range(4)], [y_copy(1, step) for step in range(3)]]
    c_copies = [c_copy(step) for step in range(NY)]

    v_copies[0][0].start()
    v_copies[1][0].start()
    loads[3].wait()
    for t in range(MAXO):
        blocks = [a_in[:, i * BLK:(i + 1) * BLK] for i in range(occ_blocks)]
        ag[c, y, x, :, t * BLK:(t + 1) * BLK] = pick(blocks, row_picks, t)
    pack(1)
    pack(3)
    for copy in x_copies:
        copy.start()
    for index in range(1, PIECES):
        for way in range(2):
            v_copies[way][index].start()

    def when(holds, action):
        if holds is True:
            action()
        elif holds is not False:
            pl.when(holds)(action)

    def far(way, index, receiver):
        if index < 3 * PIECES:
            return True
        if way == 0:
            return receiver != 0
        return True if index < 3 * PIECES + PIECES // 2 else receiver == 0

    receivers = (ring(z, 1, NZ), ring(z, -1, NZ))

    def v_pass(index):
        for way in range(2):
            if index < len(v_copies[way]):
                when(far(way, index, z), v_copies[way][index].wait_recv)
            if index + PIECES < len(v_copies[way]):
                when(far(way, index + PIECES, receivers[way]), v_copies[way][index + PIECES].start)

    def y_pass(step):
        for way in range(2):
            if step <= len(y_copies[way]):
                y_copies[way][step - 1].wait_recv()
                if step < len(y_copies[way]):
                    y_copies[way][step].start()
                c_copies[step if way == 0 else NY - step].start()

    ranks = []
    for i in range(occ_blocks):
        rank = jnp.int32(0)
        for other in range(i):
            rank = rank + jnp.where(occ_s[other] == occ_s[i], 1, 0)
        ranks.append(rank)

    def build(step):
        c_copies[step].wait_recv()
        group = ring(y, -step, NY)
        distance = ring(z, -group, NZ)
        slot = 2 * jnp.minimum(distance, NZ - distance) - jnp.where((distance > 0) & (distance <= NZ // 2), 1, 0)
        nothing = jnp.zeros((BLK, BLK), jnp.bfloat16)
        for half in range(2):
            kb = group * 2 + half
            stacked = jnp.concatenate([ag[cc, group, 2 * half + xx] for xx in range(2) for cc in range(2)], axis=0)
            turned = lax.dot_general(unit[...], stacked, (((1,), (1,)), ((), ())), preferred_element_type=jnp.float32).astype(jnp.bfloat16)
            symmetry = k_s[kb]
            for i in range(occ_blocks):
                chosen = lax.select(ranks[i] == 0, turned[:BLK], turned[BLK:])
                amask[i * BLK:(i + 1) * BLK, pl.ds(pl.multiple_of(slot * depth + half * BLK, BLK), BLK)] = lax.select(occ_s[i] == symmetry, chosen, nothing)

    def product(first, last):
        return jnp.dot(amask[:, first * depth:last * depth], vbuf[first * depth:last * depth], preferred_element_type=jnp.float32)

    diagonal = [lax.broadcasted_iota(jnp.int32, unit.shape, axis) for axis in range(2)]
    unit[...] = (diagonal[0] == diagonal[1]).astype(jnp.bfloat16)
    v_pass(0)
    for copy in x_copies:
        copy.wait_recv()
    y_copies[0][0].start()
    y_copies[1][0].start()
    c_copies[0].start()
    v_pass(1)
    v_pass(2)
    y_pass(1)
    v_pass(3)
    v_pass(4)
    y_pass(2)
    build(0)
    v_pass(5)
    y_pass(3)
    build(1)
    build(7)
    v_pass(6)
    v_pass(7)
    y_pass(4)
    build(2)
    build(6)
    v_pass(8)
    build(3)
    build(5)
    v_pass(9)
    v_pass(10)
    v_pass(11)
    build(4)
    a_last[...] = amask[:, 7 * depth:]
    acc[...] = product(0, 5)
    acc[...] += product(5, 7)
    for index in range(3 * PIECES, 4 * PIECES):
        v_pass(index)
    v_last[...] = vbuf[7 * depth:]

    for way in range(2):
        for index, copy in enumerate(v_copies[way]):
            when(far(way, index, receivers[way]), copy.wait_send)
    for copy in x_copies + y_copies[0] + y_copies[1] + c_copies:
        copy.wait_send()


def expand_kernel(occ_hbm, vir_hbm, acc, a_last, v_last, out_hbm, occ_s, vir_s, packed, full, sems):
    labels = [pltpu.make_async_copy(occ_hbm, occ_s, sems.at[0]), pltpu.make_async_copy(vir_hbm, vir_s, sems.at[1])]
    for copy in labels:
        copy.start()
    copies = []
    for i in range(occ_s.shape[0]):
        span = slice(i * BLK, (i + 1) * BLK)
        rest = jnp.dot(a_last[span, :], v_last[...], preferred_element_type=jnp.float32)
        packed[i] = (acc[span, :] + rest).astype(packed.dtype)
        if i == 0:
            for copy in labels:
                copy.wait()
        taken = jnp.int32(0)
        for j in range(vir_s.shape[0]):
            match = vir_s[j] == occ_s[i]
            slot = pl.multiple_of(jnp.minimum(taken, MAXB - 1) * BLK, BLK)
            block = packed[i, :, pl.ds(slot, BLK)]
            full[span, j * BLK:(j + 1) * BLK] = lax.select(match, block, jnp.zeros_like(block))
            taken = taken + jnp.where(match, 1, 0)
        copies.append(pltpu.make_async_copy(full.at[span], out_hbm.at[span], sems.at[2 + i]))
        copies[-1].start()
    for copy in copies:
        copy.wait()


def in_hbm(array):
    return pltpu.with_memory_space_constraint(array, pltpu.HBM)


def per_device(amplitudes, integrals, occ_sym, vir_sym, k_sym):
    occ_rows, part = amplitudes.shape
    depth, columns = integrals.shape
    width = MAXB * BLK
    bf16 = jnp.bfloat16
    vmem = pl.BlockSpec(memory_space=pltpu.VMEM)
    hbm = pl.BlockSpec(memory_space=pltpu.HBM)
    v_count = 4 * PIECES
    dma = pltpu.SemaphoreType.DMA
    occ_sym, vir_sym, k_sym = in_hbm(occ_sym), in_hbm(vir_sym), in_hbm(k_sym)
    parts = pl.pallas_call(
        ladder_kernel,
        out_shape=(pltpu.VMEM((occ_rows, width), jnp.float32), pltpu.VMEM((occ_rows, depth), bf16), pltpu.VMEM((depth, width), bf16)),
        in_specs=[hbm] * 5,
        out_specs=(vmem,) * 3,
        scratch_shapes=[
            pltpu.SMEM(occ_sym.shape, jnp.int32),
            pltpu.SMEM(vir_sym.shape, jnp.int32),
            pltpu.SMEM(k_sym.shape, jnp.int32),
            pltpu.VMEM((part, occ_rows), bf16),
            pltpu.VMEM((depth, columns), bf16),
            pltpu.VMEM((2, NY, NX, part, MAXO * BLK), bf16),
            pltpu.VMEM((NZ * depth, width), bf16),
            pltpu.VMEM((occ_rows, NZ * depth), bf16),
            pltpu.VMEM((MAXO * BLK, MAXO * BLK), bf16),
            dma((4 + PIECES,)),
            dma((2, v_count)), dma((2, v_count)),
            dma((3,)), dma((3,)),
            dma((2, 4)), dma((2, 4)),
            dma((NY,)), dma((NY,)),
        ],
        compiler_params=pltpu.CompilerParams(collective_id=0, has_side_effects=True, vmem_limit_bytes=24 << 20),
        name="ladder_ring",
    )(occ_sym, vir_sym, k_sym, in_hbm(amplitudes.T), in_hbm(integrals))
    return pl.pallas_call(
        expand_kernel,
        out_shape=jax.ShapeDtypeStruct((occ_rows, columns), bf16),
        in_specs=[hbm, hbm, vmem, vmem, vmem],
        out_specs=hbm,
        scratch_shapes=[
            pltpu.SMEM(occ_sym.shape, jnp.int32),
            pltpu.SMEM(vir_sym.shape, jnp.int32),
            pltpu.VMEM((occ_rows // BLK, BLK, width), bf16),
            pltpu.VMEM((occ_rows, columns), bf16),
            dma((2 + occ_rows // BLK,)),
        ],
        compiler_params=pltpu.CompilerParams(vmem_limit_bytes=24 << 20),
        name="expand",
    )(occ_sym, vir_sym, *parts)


def solution(mesh):
    return jax.shard_map(
        per_device,
        mesh=mesh,
        in_specs=(P("occ", "vir"), P("occ", "vir"), P("occ"), P("vir"), P()),
        out_specs=P("occ", "vir"),
        check_vma=False,
    )
```

time: 46.1 us -> 43.5 us (0.944); the launches traced: 46 us -> 42.7 us
  Pallas kernels: 46 us -> 42.7 us
    pallas_call x1, Pallas kernels: 43.1 us -> 39.5 us  [per_device(): pl.pallas_call(ladder_kernel, out_shape=(pltpu.VMEM((occ_rows, width), jn...]
where the time goes in v3:
time: 43.5 us; the launch traced here: 42.7 us
  Pallas kernels  42.7 us (98%)
    pallas_call x1, Pallas kernels, per_device(): pl.pallas_call(ladder_kernel, out_shape=(pltpu.VMEM((occ_rows, width), jn...  39.5 us
    pallas_call x1, Pallas kernels, per_device(): pl.pallas_call(expand_kernel, out_shape=jax.ShapeDtypeStruct((occ_rows, c...  3.19 us

profile of v3, /device:TPU:1, one launch (start us, length us, event | category | flops | bytes accessed | tf_op | source)
XLA Modules:
  0.0 42.7 jit_solution(3353219171362219697)
XLA Ops:
  0.0 39.5 %ladder_ring.1 = (f32[768,640]{1,0:T(8,128)S(1)}, bf16[768,256]{1,0:T(8,128)(2,1)S(1)}, bf16[256,640]{1,0:T(8,128)(2,1)S(1)}) custom-call(s32[6]{0:T(128)} %occ_hbm.3, s32[20]{0:T(128)} %vir_hbm.3, s32[16]{0:T(128)} %k_hbm.1, bf16[32,768]{1,0:T(8,128)(2,1)} %bitcast.1, bf16[256,2560]{1,0:T(8,128)(2,1)} %v_hbm.1), custom_call_target="tpu_custom_call" | custom-call | tf_op jit(solution)/shard_map/ladder_ring/pallas_call | solution.py:273
  39.5 3.2 %expand.1 = bf16[768,2560]{1,0:T(8,128)(2,1)} custom-call(s32[6]{0:T(128)} %occ_hbm.3, s32[20]{0:T(128)} %vir_hbm.3, f32[768,640]{1,0:T(8,128)S(1)} %get-tuple-element.8.acc, bf16[768,256]{1,0:T(8,128)(2,1)S(1)} %get-tuple-element.9.a_last, bf16[256,640]{1,0:T(8,128)(2,1)S(1)} %get-tuple-element.10.v_last), custom_call_target="tpu_custom_call" | custom-call | tf_op jit(solution)/shard_map/expand/pallas_call | solution.py:297

commit v4 on v3

--- a/solution.py
+++ b/solution.py
@@ -10,6 +10,8 @@
 MAXB = 5
 NZ, NY, NX = 8, 8, 4
 PIECES = 4
+FIRST_ORDER = "v1vv2v3vv4vxvvcbbvbbvbbvbb"
+ORDER = "v1vv2v3vv4vvxvvvvcbbbbbbbb"
 MESH = pl.DeviceIdType.MESH
 
 
@@ -96,37 +98,44 @@
     v_counts = (3 * PIECES + PIECES // 2, 4 * PIECES)
     v_copies = [[v_copy(way, index) for index in range(v_counts[way])] for way in range(2)]
 
-    def x_copy(step):
-        return pltpu.make_async_remote_copy(
-            src_ref=ag.at[c, y, x], dst_ref=ag.at[c, y, x], send_sem=xsend.at[step - 1], recv_sem=xrecv.at[step - 1],
-            device_id=x_far[step], device_id_type=MESH)
-
     def y_copy(way, step):
         group = ring(y, -step if way == 0 else step, NY)
         return pltpu.make_async_remote_copy(
-            src_ref=ag.at[c, group], dst_ref=ag.at[c, group], send_sem=ysend.at[way, step], recv_sem=yrecv.at[way, step],
+            src_ref=ag.at[c, x, group], dst_ref=ag.at[c, x, group], send_sem=ysend.at[way, step], recv_sem=yrecv.at[way, step],
             device_id=(y_next, y_prev)[way], device_id_type=MESH)
 
+    def x_copy(step, group):
+        part_of = ag.at[c, x] if group is None else ag.at[c, x, group]
+        return pltpu.make_async_remote_copy(
+            src_ref=part_of, dst_ref=part_of, send_sem=xsend.at[step - 1], recv_sem=xrecv.at[step - 1],
+            device_id=x_far[step], device_id_type=MESH)
+
     def c_copy(step):
-        group = ring(y, -step, NY)
+        column = ring(x, step, NX)
         return pltpu.make_async_remote_copy(
-            src_ref=ag.at[c, group], dst_ref=ag.at[c, group], send_sem=csend.at[step], recv_sem=crecv.at[step],
+            src_ref=ag.at[c, column], dst_ref=ag.at[c, column], send_sem=csend.at[step], recv_sem=crecv.at[step],
             device_id=twin, device_id_type=MESH)
 
-    x_copies = [x_copy(step) for step in (1, 3, 2)]
     y_copies = [[y_copy(0, step) for step in range(4)], [y_copy(1, step) for step in range(3)]]
-    c_copies = [c_copy(step) for step in range(NY)]
+    x_whole = [x_copy(step, None) for step in (1, 3, 2)]
+    c_copies = [c_copy(step) for step in range(NX)]
+
+    def x_send(step):
+        group = ring(y, step, NY)
+        for target in (1, 3, 2):
+            x_copy(target, group).start()
 
     v_copies[0][0].start()
     v_copies[1][0].start()
     loads[3].wait()
     for t in range(MAXO):
         blocks = [a_in[:, i * BLK:(i + 1) * BLK] for i in range(occ_blocks)]
-        ag[c, y, x, :, t * BLK:(t + 1) * BLK] = pick(blocks, row_picks, t)
+        ag[c, x, y, :, t * BLK:(t + 1) * BLK] = pick(blocks, row_picks, t)
     pack(1)
     pack(3)
-    for copy in x_copies:
-        copy.start()
+    y_copies[0][0].start()
+    y_copies[1][0].start()
+    x_send(0)
     for index in range(1, PIECES):
         for way in range(2):
             v_copies[way][index].start()
@@ -147,7 +156,7 @@
     receivers = (ring(z, 1, NZ), ring(z, -1, NZ))
 
     def v_pass(index):
-        for way in range(2):
+        for way in (1, 0):
             if index < len(v_copies[way]):
                 when(far(way, index, z), v_copies[way][index].wait_recv)
             if index + PIECES < len(v_copies[way]):
@@ -159,7 +168,9 @@
                 y_copies[way][step - 1].wait_recv()
                 if step < len(y_copies[way]):
                     y_copies[way][step].start()
-                c_copies[step if way == 0 else NY - step].start()
+                x_send(-step if way == 0 else step)
+        if step == NY // 2:
+            c_copies[0].start()
 
     ranks = []
     for i in range(occ_blocks):
@@ -169,14 +180,13 @@
         ranks.append(rank)
 
     def build(step):
-        c_copies[step].wait_recv()
         group = ring(y, -step, NY)
         distance = ring(z, -group, NZ)
         slot = 2 * jnp.minimum(distance, NZ - distance) - jnp.where((distance > 0) & (distance <= NZ // 2), 1, 0)
         nothing = jnp.zeros((BLK, BLK), jnp.bfloat16)
         for half in range(2):
             kb = group * 2 + half
-            stacked = jnp.concatenate([ag[cc, group, 2 * half + xx] for xx in range(2) for cc in range(2)], axis=0)
+            stacked = jnp.concatenate([ag[cc, 2 * half + xx, group] for xx in range(2) for cc in range(2)], axis=0)
             turned = lax.dot_general(unit[...], stacked, (((1,), (1,)), ((), ())), preferred_element_type=jnp.float32).astype(jnp.bfloat16)
             symmetry = k_s[kb]
             for i in range(occ_blocks):
@@ -188,38 +198,34 @@
 
     diagonal = [lax.broadcasted_iota(jnp.int32, unit.shape, axis) for axis in range(2)]
     unit[...] = (diagonal[0] == diagonal[1]).astype(jnp.bfloat16)
-    v_pass(0)
-    for copy in x_copies:
-        copy.wait_recv()
-    y_copies[0][0].start()
-    y_copies[1][0].start()
-    c_copies[0].start()
-    v_pass(1)
-    v_pass(2)
-    y_pass(1)
-    v_pass(3)
-    v_pass(4)
-    y_pass(2)
-    build(0)
-    v_pass(5)
-    y_pass(3)
-    build(1)
-    build(7)
-    v_pass(6)
-    v_pass(7)
-    y_pass(4)
-    build(2)
-    build(6)
-    v_pass(8)
-    build(3)
-    build(5)
-    v_pass(9)
-    v_pass(10)
-    v_pass(11)
-    build(4)
+    def x_pass():
+        for copy in x_whole:
+            copy.wait_recv()
+        for copy in c_copies[1:]:
+            copy.start()
+
+    def c_pass():
+        for copy in c_copies:
+            copy.wait_recv()
+
+    def run(order):
+        ring_steps, builds = iter(range(4 * PIECES)), iter((0, 1, 7, 2, 6, 3, 5, 4))
+        for event in order:
+            if event == "v":
+                v_pass(next(ring_steps))
+            elif event == "x":
+                x_pass()
+            elif event == "c":
+                c_pass()
+            elif event == "b":
+                build(next(builds))
+            else:
+                y_pass(int(event))
+
+    pl.when(z == 0)(lambda: run(FIRST_ORDER))
+    pl.when(z != 0)(lambda: run(ORDER))
     a_last[...] = amask[:, 7 * depth:]
-    acc[...] = product(0, 5)
-    acc[...] += product(5, 7)
+    acc[...] = product(0, 7)
     for index in range(3 * PIECES, 4 * PIECES):
         v_pass(index)
     v_last[...] = vbuf[7 * depth:]
@@ -227,7 +233,7 @@
     for way in range(2):
         for index, copy in enumerate(v_copies[way]):
             when(far(way, index, receivers[way]), copy.wait_send)
-    for copy in x_copies + y_copies[0] + y_copies[1] + c_copies:
+    for copy in x_whole + y_copies[0] + y_copies[1] + c_copies:
         copy.wait_send()
 
 
@@ -281,7 +287,7 @@
             pltpu.SMEM(k_sym.shape, jnp.int32),
             pltpu.VMEM((part, occ_rows), bf16),
             pltpu.VMEM((depth, columns), bf16),
-            pltpu.VMEM((2, NY, NX, part, MAXO * BLK), bf16),
+            pltpu.VMEM((2, NX, NY, part, MAXO * BLK), bf16),
             pltpu.VMEM((NZ * depth, width), bf16),
             pltpu.VMEM((occ_rows, NZ * depth), bf16),
             pltpu.VMEM((MAXO * BLK, MAXO * BLK), bf16),
@@ -289,7 +295,7 @@
             dma((2, v_count)), dma((2, v_count)),
             dma((3,)), dma((3,)),
             dma((2, 4)), dma((2, 4)),
-            dma((NY,)), dma((NY,)),
+            dma((NX,)), dma((NX,)),
         ],
         compiler_params=pltpu.CompilerParams(collective_id=0, has_side_effects=True, vmem_limit_bytes=24 << 20),
         name="ladder_ring",

time: 43.5 us -> 42.2 us (0.970); the launches traced: 42.7 us -> 42.1 us
  Pallas kernels: 42.7 us -> 42.1 us
    pallas_call x1, Pallas kernels: 39.5 us -> 38.9 us  [per_device(): pl.pallas_call(ladder_kernel, out_shape=(pltpu.VMEM((occ_rows, width), jn...]
where the time goes in v4:
time: 42.2 us; the launch traced here: 42.1 us
  Pallas kernels  42.1 us (100%)
    pallas_call x1, Pallas kernels, per_device(): pl.pallas_call(ladder_kernel, out_shape=(pltpu.VMEM((occ_rows, width), jn...  38.9 us
    pallas_call x1, Pallas kernels, per_device(): pl.pallas_call(expand_kernel, out_shape=jax.ShapeDtypeStruct((occ_rows, c...  3.17 us

profile of v4, /device:TPU:1, one launch (start us, length us, event | category | flops | bytes accessed | tf_op | source)
XLA Modules:
  0.0 42.1 jit_solution(2523866282454741848)
XLA Ops:
  0.0 38.9 %ladder_ring.1 = (f32[768,640]{1,0:T(8,128)S(1)}, bf16[768,256]{1,0:T(8,128)(2,1)S(1)}, bf16[256,640]{1,0:T(8,128)(2,1)S(1)}) custom-call(s32[6]{0:T(128)} %occ_hbm.3, s32[20]{0:T(128)} %vir_hbm.3, s32[16]{0:T(128)} %k_hbm.1, bf16[32,768]{1,0:T(8,128)(2,1)} %bitcast.1, bf16[256,2560]{1,0:T(8,128)(2,1)} %v_hbm.1), custom_call_target="tpu_custom_call" | custom-call | tf_op jit(solution)/shard_map/ladder_ring/pallas_call | solution.py:279
  38.9 3.2 %expand.1 = bf16[768,2560]{1,0:T(8,128)(2,1)} custom-call(s32[6]{0:T(128)} %occ_hbm.3, s32[20]{0:T(128)} %vir_hbm.3, f32[768,640]{1,0:T(8,128)S(1)} %get-tuple-element.8.acc, bf16[768,256]{1,0:T(8,128)(2,1)S(1)} %get-tuple-element.9.a_last, bf16[256,640]{1,0:T(8,128)(2,1)S(1)} %get-tuple-element.10.v_last), custom_call_target="tpu_custom_call" | custom-call | tf_op jit(solution)/shard_map/expand/pallas_call | solution.py:303

commit v5 on v4

--- a/solution.py
+++ b/solution.py
@@ -15,7 +15,7 @@
 MESH = pl.DeviceIdType.MESH
 
 
-def ladder_kernel(occ_hbm, vir_hbm, k_hbm, a_hbm, v_hbm, acc, a_last, v_last, occ_s, vir_s, k_s, a_in, v_in, ag, vbuf, amask, unit,
+def ladder_kernel(occ_hbm, vir_hbm, k_hbm, a_hbm, v_hbm, acc, a_last, v_last, occ_out, vir_out, occ_s, vir_s, k_s, a_in, v_in, ag, vbuf, amask, unit,
                   in_sem, vsend, vrecv, xsend, xrecv, ysend, yrecv, csend, crecv):
     occ_rows = acc.shape[0]
     occ_blocks = occ_rows // BLK
@@ -196,6 +196,10 @@
     def product(first, last):
         return jnp.dot(amask[:, first * depth:last * depth], vbuf[first * depth:last * depth], preferred_element_type=jnp.float32)
 
+    for i in range(occ_blocks):
+        occ_out[i] = occ_s[i]
+    for j in range(vir_blocks):
+        vir_out[j] = vir_s[j]
     diagonal = [lax.broadcasted_iota(jnp.int32, unit.shape, axis) for axis in range(2)]
     unit[...] = (diagonal[0] == diagonal[1]).astype(jnp.bfloat16)
     def x_pass():
@@ -237,18 +241,12 @@
         copy.wait_send()
 
 
-def expand_kernel(occ_hbm, vir_hbm, acc, a_last, v_last, out_hbm, occ_s, vir_s, packed, full, sems):
-    labels = [pltpu.make_async_copy(occ_hbm, occ_s, sems.at[0]), pltpu.make_async_copy(vir_hbm, vir_s, sems.at[1])]
-    for copy in labels:
-        copy.start()
+def expand_kernel(acc, a_last, v_last, occ_s, vir_s, out_hbm, packed, full, sems):
     copies = []
     for i in range(occ_s.shape[0]):
         span = slice(i * BLK, (i + 1) * BLK)
         rest = jnp.dot(a_last[span, :], v_last[...], preferred_element_type=jnp.float32)
         packed[i] = (acc[span, :] + rest).astype(packed.dtype)
-        if i == 0:
-            for copy in labels:
-                copy.wait()
         taken = jnp.int32(0)
         for j in range(vir_s.shape[0]):
             match = vir_s[j] == occ_s[i]
@@ -273,14 +271,15 @@
     bf16 = jnp.bfloat16
     vmem = pl.BlockSpec(memory_space=pltpu.VMEM)
     hbm = pl.BlockSpec(memory_space=pltpu.HBM)
+    smem = pl.BlockSpec(memory_space=pltpu.SMEM)
     v_count = 4 * PIECES
     dma = pltpu.SemaphoreType.DMA
     occ_sym, vir_sym, k_sym = in_hbm(occ_sym), in_hbm(vir_sym), in_hbm(k_sym)
     parts = pl.pallas_call(
         ladder_kernel,
-        out_shape=(pltpu.VMEM((occ_rows, width), jnp.float32), pltpu.VMEM((occ_rows, depth), bf16), pltpu.VMEM((depth, width), bf16)),
+        out_shape=(pltpu.VMEM((occ_rows, width), jnp.float32), pltpu.VMEM((occ_rows, depth), bf16), pltpu.VMEM((depth, width), bf16), pltpu.SMEM(occ_sym.shape, jnp.int32), pltpu.SMEM(vir_sym.shape, jnp.int32)),
         in_specs=[hbm] * 5,
-        out_specs=(vmem,) * 3,
+        out_specs=(vmem,) * 3 + (smem,) * 2,
         scratch_shapes=[
             pltpu.SMEM(occ_sym.shape, jnp.int32),
             pltpu.SMEM(vir_sym.shape, jnp.int32),
@@ -303,18 +302,16 @@
     return pl.pallas_call(
         expand_kernel,
         out_shape=jax.ShapeDtypeStruct((occ_rows, columns), bf16),
-        in_specs=[hbm, hbm, vmem, vmem, vmem],
+        in_specs=[vmem, vmem, vmem, smem, smem],
         out_specs=hbm,
         scratch_shapes=[
-            pltpu.SMEM(occ_sym.shape, jnp.int32),
-            pltpu.SMEM(vir_sym.shape, jnp.int32),
             pltpu.VMEM((occ_rows // BLK, BLK, width), bf16),
             pltpu.VMEM((occ_rows, columns), bf16),
             dma((2 + occ_rows // BLK,)),
         ],
         compiler_params=pltpu.CompilerParams(vmem_limit_bytes=24 << 20),
         name="expand",
-    )(occ_sym, vir_sym, *parts)
+    )(*parts)
 
 
 def solution(mesh):

time: 42.2 us -> 41.7 us (0.988)
  Pallas kernels: 42.1 us -> 41.6 us
    pallas_call x1, Pallas kernels: 3.17 us -> 2.69 us  [per_device(): pl.pallas_call(expand_kernel, out_shape=jax.ShapeDtypeStruct((occ_rows, c...]
where the time goes in v5:
time: 41.7 us; the launch traced here: 41.6 us
  Pallas kernels  41.6 us (100%)
    pallas_call x1, Pallas kernels, per_device(): pl.pallas_call(ladder_kernel, out_shape=(pltpu.VMEM((occ_rows, width), jn...  38.9 us
    pallas_call x1, Pallas kernels, per_device(): pl.pallas_call(expand_kernel, out_shape=jax.ShapeDtypeStruct((occ_rows, c...  2.69 us

profile of v5, /device:TPU:1, one launch (start us, length us, event | category | flops | bytes accessed | tf_op | source)
XLA Modules:
  0.0 41.6 jit_solution(7917900773277307254)
XLA Ops:
  0.0 38.9 %ladder_ring.1 = (f32[768,640]{1,0:T(8,128)S(1)}, bf16[768,256]{1,0:T(8,128)(2,1)S(1)}, bf16[256,640]{1,0:T(8,128)(2,1)S(1)}, s32[6]{0:T(128)S(4)}, s32[20]{0:T(128)S(4)}) custom-call(s32[6]{0:T(128)} %occ_hbm.1, s32[20]{0:T(128)} %vir_hbm.1, s32[16]{0:T(128)} %k_hbm.1, bf16[32,768]{1,0:T(8,128)(2,1)} %bitcast.1, bf16[256,2560]{1,0:T(8,128)(2,1)} %v_hbm.1), custom_call_target="tpu_custom_call" | custom-call | tf_op jit(solution)/shard_map/ladder_ring/pallas_call | solution.py:278
  38.9 2.7 %expand.1 = bf16[768,2560]{1,0:T(8,128)(2,1)} custom-call(f32[768,640]{1,0:T(8,128)S(1)} %get-tuple-element.10.acc, bf16[768,256]{1,0:T(8,128)(2,1)S(1)} %get-tuple-element.11.a_last, bf16[256,640]{1,0:T(8,128)(2,1)S(1)} %get-tuple-element.12.v_last, s32[6]{0:T(128)S(4)} %get-tuple-element.13.occ_s, s32[20]{0:T(128)S(4)} %get-tuple-element.14.vir_s), custom_call_target="tpu_custom_call" | custom-call | tf_op jit(solution)/shard_map/expand/pallas_call | solution.py:302

commit v6 on v5

--- a/solution.py
+++ b/solution.py
@@ -10,7 +10,7 @@
 MAXB = 5
 NZ, NY, NX = 8, 8, 4
 PIECES = 4
-FIRST_ORDER = "v1vv2v3vv4vxvvcbbvbbvbbvbb"
+FIRST_ORDER = "v1vv2v3vv4vxvvvcbbbvbbvbbb"
 ORDER = "v1vv2v3vv4vvxvvvvcbbbbbbbb"
 MESH = pl.DeviceIdType.MESH
 

time: 41.7 us -> 41.5 us (level)
  no operation moved by 1% of the time
where the time goes in v6:
time: 41.5 us; the launch traced here: 41.4 us
  Pallas kernels  41.4 us (100%)
    pallas_call x1, Pallas kernels, per_device(): pl.pallas_call(ladder_kernel, out_shape=(pltpu.VMEM((occ_rows, width), jn...  38.7 us
    pallas_call x1, Pallas kernels, per_device(): pl.pallas_call(expand_kernel, out_shape=jax.ShapeDtypeStruct((occ_rows, c...  2.69 us

profile of v6, /device:TPU:1, one launch (start us, length us, event | category | flops | bytes accessed | tf_op | source)
XLA Modules:
  0.0 41.4 jit_solution(4805512287777327445)
XLA Ops:
  0.0 38.7 %ladder_ring.1 = (f32[768,640]{1,0:T(8,128)S(1)}, bf16[768,256]{1,0:T(8,128)(2,1)S(1)}, bf16[256,640]{1,0:T(8,128)(2,1)S(1)}, s32[6]{0:T(128)S(4)}, s32[20]{0:T(128)S(4)}) custom-call(s32[6]{0:T(128)} %occ_hbm.1, s32[20]{0:T(128)} %vir_hbm.1, s32[16]{0:T(128)} %k_hbm.1, bf16[32,768]{1,0:T(8,128)(2,1)} %bitcast.1, bf16[256,2560]{1,0:T(8,128)(2,1)} %v_hbm.1), custom_call_target="tpu_custom_call" | custom-call | tf_op jit(solution)/shard_map/ladder_ring/pallas_call | solution.py:278
  38.7 2.7 %expand.1 = bf16[768,2560]{1,0:T(8,128)(2,1)} custom-call(f32[768,640]{1,0:T(8,128)S(1)} %get-tuple-element.10.acc, bf16[768,256]{1,0:T(8,128)(2,1)S(1)} %get-tuple-element.11.a_last, bf16[256,640]{1,0:T(8,128)(2,1)S(1)} %get-tuple-element.12.v_last, s32[6]{0:T(128)S(4)} %get-tuple-element.13.occ_s, s32[20]{0:T(128)S(4)} %get-tuple-element.14.vir_s), custom_call_target="tpu_custom_call" | custom-call | tf_op jit(solution)/shard_map/expand/pallas_call | solution.py:302
